TPU v7x, 32 devices: a whole 2x2x4 slice. The times are simulated.
32 devices in a mesh: fsdp: 8 (over z, x), seq: 4 (over y, core).
Axes of the slice: x: 2, y: 2, z: 4, core: 2. Of those that a mesh axis runs over, the one named last changes fastest.
Arguments:
- residual: bfloat16 [24, 1024, 767], P('fsdp', 'seq'), may hold values from -6 to 6
- out_grad: bfloat16 [24, 1024, 767], P('fsdp', 'seq'), may hold values from -6 to 6
- doc_lengths: int32 [24, 8], P('fsdp'), may hold values from 1 to 512, 1024 in all within a row
- gain_one: float32 [768], replicated, may hold values from 0.5 to 1.5
- qkv_weight: float32 [768, 2304], P('fsdp'), may hold values from -0.21875 to 0.21875
- qv_bias: float32 [12, 128], replicated, may hold values from -3 to 3
- out_weight: float32 [768, 767], P('fsdp'), may hold values from -0.875 to 0.875
- out_bias: float32 [767], replicated, may hold values from -3 to 3
- gain_two: float32 [768], replicated, may hold values from 0.5 to 1.5
- fc_weight: float32 [768, 3072], P('fsdp'), may hold values from -0.21875 to 0.21875
- fc_bias: float32 [3072], replicated, may hold values from -3 to 3
- proj_weight: float32 [3072, 767], P('fsdp'), may hold values from -0.15625 to 0.15625
- proj_bias: float32 [767], replicated, may hold values from -3 to 3
Outputs:
- output: bfloat16 [24, 1024, 767], P('fsdp', 'seq')
- input_grad: float32 [24, 1024, 767], P('fsdp', 'seq')
- gain_one_grad: float32 [768], replicated
- qkv_weight_grad: float32 [768, 2304], P('fsdp')
- qv_bias_grad: float32 [12, 128], replicated
- out_weight_grad: float32 [768, 767], P('fsdp')
- out_bias_grad: float32 [767], replicated
- gain_two_grad: float32 [768], replicated
- fc_weight_grad: float32 [768, 3072], P('fsdp')
- fc_bias_grad: float32 [3072], replicated
- proj_weight_grad: float32 [3072, 767], P('fsdp')
- proj_bias_grad: float32 [767], replicated
Inputs may be any that keep to these rules, and one draw needn't show every extreme that they name: `doc_lengths`: each sequence's 8 document lengths sum to 1024; the longest is exactly 512 tokens.
All inputs are finite; a program needn't handle non-finite values.
Results may differ from a plain program's by a relative error of at most 0.014.
Values may be sent and summed in bfloat16 or wider, within the bound.
No kernel may reach another device: no remote copies, remote signals or barrier semaphores. Data moves between devices by JAX's collectives and lax.ppermute only.
A program may use at most 320 MiB of HBM per device.

v0:
```python
import functools
import jax
import jax.numpy as jnp
from jax import lax
from jax.sharding import PartitionSpec as P

EPS = 1e-06


def centred_norm(residual, gain):
    row_total = jnp.sum(residual, axis=-1, keepdims=True)
    full_row = jnp.concatenate([residual, -row_total], axis=-1)
    inv_rms = lax.rsqrt(jnp.mean(full_row * full_row, axis=-1, keepdims=True) + EPS)
    return full_row * inv_rms * gain


def document_index(lengths, length):
    starts = jnp.cumsum(lengths, axis=1) - lengths
    position = jnp.arange(length, dtype=jnp.int32)
    inside = (position[None, :, None] >= starts[:, None, :]).astype(jnp.int32)
    return jnp.sum(inside, axis=2) - 1


def masked_scores(queries, key_rows, doc_ids, first_row, row_count, factor):
    scores = factor * jnp.einsum(
        "bqhe,bkhe->bhqk", queries, key_rows, preferred_element_type=jnp.float32
    )
    length = key_rows.shape[1]
    row_pos = first_row + jnp.arange(row_count, dtype=jnp.int32)
    col_pos = jnp.arange(length, dtype=jnp.int32)
    row_ids = doc_ids[:, first_row : first_row + row_count]
    allowed = (row_ids[:, :, None] == doc_ids[:, None, :]) & (
        col_pos[None, None, :] <= row_pos[None, :, None]
    )
    return jnp.where(allowed[:, None], scores, -1e30)


def local(
    residual,
    out_grad,
    doc_lengths,
    gain_one,
    qkv_weight,
    qv_bias,
    out_weight,
    out_bias,
    gain_two,
    fc_weight,
    fc_bias,
    proj_weight,
    proj_bias,
):
    ranks = lax.axis_size("seq")
    seq_count, local_len, narrow = residual.shape
    width = narrow + 1
    full_len = local_len * ranks
    heads_all = qv_bias.shape[0]
    head_dim = qv_bias.shape[1] // 2
    my_heads = heads_all // ranks
    token_count = seq_count * local_len
    factor = head_dim ** (-0.5)
    block_rows = min(512, full_len)
    qkv_matrix, out_matrix, fc_matrix, proj_matrix = (
        lax.all_gather(qkv_weight.astype(jnp.bfloat16), "fsdp", axis=0, tiled=True),
        lax.all_gather(out_weight.astype(jnp.bfloat16), "fsdp", axis=0, tiled=True),
        lax.all_gather(fc_weight.astype(jnp.bfloat16), "fsdp", axis=0, tiled=True),
        lax.all_gather(proj_weight.astype(jnp.bfloat16), "fsdp", axis=0, tiled=True),
    )
    resid_flat = residual.astype(jnp.float32).reshape(token_count, narrow)
    normed_one = centred_norm(resid_flat, gain_one).astype(jnp.bfloat16)
    zero_part = jnp.zeros((heads_all, head_dim), jnp.float32)
    bias_full = jnp.stack(
        [qv_bias[:, :head_dim], zero_part, qv_bias[:, head_dim:]], axis=1
    ).reshape(3 * width)
    packed = (
        jnp.dot(normed_one, qkv_matrix, preferred_element_type=jnp.float32) + bias_full
    ).astype(jnp.bfloat16)
    packed = packed.reshape(seq_count, local_len, ranks, my_heads * 3 * head_dim)
    by_heads = lax.all_to_all(packed, "seq", split_axis=2, concat_axis=1, tiled=True)
    by_heads = by_heads.reshape(seq_count, full_len, my_heads, 3, head_dim)
    queries = by_heads[:, :, :, 0]
    key_rows = by_heads[:, :, :, 1]
    value_rows = by_heads[:, :, :, 2]
    doc_ids = document_index(doc_lengths, full_len)
    outputs_list = []
    lse_list = []
    for first_row in range(0, full_len, block_rows):
        scores = masked_scores(
            queries[:, first_row : first_row + block_rows],
            key_rows,
            doc_ids,
            first_row,
            block_rows,
            factor,
        )
        row_max = jnp.max(scores, axis=-1, keepdims=True)
        exp_scores = jnp.exp(scores - row_max)
        row_total = jnp.sum(exp_scores, axis=-1, keepdims=True)
        prob_low = (exp_scores / row_total).astype(jnp.bfloat16)
        lse_list.append(row_max + jnp.log(row_total))
        outputs_list.append(
            jnp.einsum("bhqk,bkhe->bqhe", prob_low, value_rows, preferred_element_type=jnp.float32)
        )
    attended = jnp.concatenate(outputs_list, axis=1).astype(jnp.bfloat16)
    attended = attended.reshape(seq_count, full_len, my_heads * head_dim)
    by_tokens = lax.all_to_all(attended, "seq", split_axis=1, concat_axis=2, tiled=True)
    attn_flat = by_tokens.reshape(token_count, width)
    middle = (
        resid_flat + jnp.dot(attn_flat, out_matrix, preferred_element_type=jnp.float32) + out_bias
    )
    normed_two = centred_norm(middle, gain_two).astype(jnp.bfloat16)
    pre_act = jnp.dot(normed_two, fc_matrix, preferred_element_type=jnp.float32) + fc_bias
    hidden = jax.nn.gelu(pre_act, approximate=True).astype(jnp.bfloat16)
    output = middle + jnp.dot(hidden, proj_matrix, preferred_element_type=jnp.float32) + proj_bias
    output = output.astype(jnp.bfloat16).reshape(seq_count, local_len, narrow)
    qkv_matrix, out_matrix, fc_matrix, proj_matrix = (
        lax.all_gather(qkv_weight.astype(jnp.bfloat16), "fsdp", axis=0, tiled=True),
        lax.all_gather(out_weight.astype(jnp.bfloat16), "fsdp", axis=0, tiled=True),
        lax.all_gather(fc_weight.astype(jnp.bfloat16), "fsdp", axis=0, tiled=True),
        lax.all_gather(proj_weight.astype(jnp.bfloat16), "fsdp", axis=0, tiled=True),
    )
    grad_low = out_grad.reshape(token_count, narrow)
    grad_flat = grad_low.astype(jnp.float32)
    proj_grad = jnp.einsum("tf,tc->fc", hidden, grad_low, preferred_element_type=jnp.float32)
    proj_bias_grad = jnp.sum(grad_flat, axis=0)
    d_hidden = jnp.einsum("tc,fc->tf", grad_low, proj_matrix, preferred_element_type=jnp.float32)
    gelu_value, gelu_back = jax.vjp(functools.partial(jax.nn.gelu, approximate=True), pre_act)
    d_pre = gelu_back(d_hidden)[0].astype(jnp.bfloat16)
    fc_grad = jnp.einsum("td,tf->df", normed_two, d_pre, preferred_element_type=jnp.float32)
    fc_bias_grad = jnp.sum(d_pre.astype(jnp.float32), axis=0)
    d_norm_two = jnp.einsum("tf,df->td", d_pre, fc_matrix, preferred_element_type=jnp.float32)
    second_value, second_back = jax.vjp(centred_norm, middle, gain_two)
    d_mid_part, gain_two_grad = second_back(d_norm_two)
    d_middle = grad_flat + d_mid_part
    d_branch = d_middle.astype(jnp.bfloat16)
    out_weight_part = jnp.einsum(
        "td,tc->dc", attn_flat, d_branch, preferred_element_type=jnp.float32
    )
    out_bias_grad = jnp.sum(d_branch.astype(jnp.float32), axis=0)
    d_attn = jnp.einsum(
        "tc,dc->td", d_branch, out_matrix, preferred_element_type=jnp.float32
    ).astype(jnp.bfloat16)
    d_attn = d_attn.reshape(seq_count, local_len, ranks, my_heads * head_dim)
    d_heads = lax.all_to_all(d_attn, "seq", split_axis=2, concat_axis=1, tiled=True)
    d_heads = d_heads.reshape(seq_count, full_len, my_heads, head_dim)
    key_grad = jnp.zeros((seq_count, full_len, my_heads, head_dim), jnp.float32)
    value_grad = jnp.zeros((seq_count, full_len, my_heads, head_dim), jnp.float32)
    query_parts = []
    for block_index, first_row in enumerate(range(0, full_len, block_rows)):
        query_block = queries[:, first_row : first_row + block_rows]
        grad_block = d_heads[:, first_row : first_row + block_rows]
        scores = masked_scores(query_block, key_rows, doc_ids, first_row, block_rows, factor)
        prob_full = jnp.exp(scores - lse_list[block_index])
        prob_low = prob_full.astype(jnp.bfloat16)
        d_probs = jnp.einsum(
            "bqhe,bkhe->bhqk", grad_block, value_rows, preferred_element_type=jnp.float32
        )
        row_delta = jnp.sum(prob_full * d_probs, axis=-1, keepdims=True)
        d_scores = (prob_full * (d_probs - row_delta)).astype(jnp.bfloat16)
        query_parts.append(
            factor
            * jnp.einsum("bhqk,bkhe->bqhe", d_scores, key_rows, preferred_element_type=jnp.float32)
        )
        key_grad = key_grad + factor * jnp.einsum(
            "bhqk,bqhe->bkhe", d_scores, query_block, preferred_element_type=jnp.float32
        )
        value_grad = value_grad + jnp.einsum(
            "bhqk,bqhe->bkhe", prob_low, grad_block, preferred_element_type=jnp.float32
        )
    query_grad = jnp.concatenate(query_parts, axis=1)
    d_packed = jnp.stack([query_grad, key_grad, value_grad], axis=3).astype(jnp.bfloat16)
    d_packed = d_packed.reshape(seq_count, full_len, my_heads * 3 * head_dim)
    d_tokens = lax.all_to_all(d_packed, "seq", split_axis=1, concat_axis=2, tiled=True)
    d_tokens = d_tokens.reshape(token_count, 3 * width)
    qkv_grad = jnp.einsum("td,tc->dc", normed_one, d_tokens, preferred_element_type=jnp.float32)
    column_sums = jnp.sum(d_tokens.astype(jnp.float32), axis=0).reshape(heads_all, 3, head_dim)
    qv_bias_grad = jnp.concatenate([column_sums[:, 0], column_sums[:, 2]], axis=1)
    d_norm_one = jnp.einsum("tc,dc->td", d_tokens, qkv_matrix, preferred_element_type=jnp.float32)
    first_value, first_back = jax.vjp(centred_norm, resid_flat, gain_one)
    d_resid_part, gain_one_grad = first_back(d_norm_one)
    input_grad = (d_middle + d_resid_part).reshape(seq_count, local_len, narrow)
    qkv_share, out_share, fc_share, proj_share = (
        lax.psum_scatter(qkv_grad, "fsdp", scatter_dimension=0, tiled=True),
        lax.psum_scatter(out_weight_part, "fsdp", scatter_dimension=0, tiled=True),
        lax.psum_scatter(fc_grad, "fsdp", scatter_dimension=0, tiled=True),
        lax.psum_scatter(proj_grad, "fsdp", scatter_dimension=0, tiled=True),
    )
    qkv_share, out_share, fc_share, proj_share = (
        lax.psum(qkv_share.astype(jnp.bfloat16), "seq").astype(jnp.float32),
        lax.psum(out_share.astype(jnp.bfloat16), "seq").astype(jnp.float32),
        lax.psum(fc_share.astype(jnp.bfloat16), "seq").astype(jnp.float32),
        lax.psum(proj_share.astype(jnp.bfloat16), "seq").astype(jnp.float32),
    )
    vector_sums = lax.psum(
        (gain_one_grad, qv_bias_grad, out_bias_grad, gain_two_grad, fc_bias_grad, proj_bias_grad),
        ("fsdp", "seq"),
    )
    return (
        output,
        input_grad,
        vector_sums[0],
        qkv_share,
        vector_sums[1],
        out_share,
        vector_sums[2],
        vector_sums[3],
        fc_share,
        vector_sums[4],
        proj_share,
        vector_sums[5],
    )


def solution(mesh):
    return jax.shard_map(
        local,
        mesh=mesh,
        in_specs=(
            P("fsdp", "seq", None),
            P("fsdp", "seq", None),
            P("fsdp", None),
            P(),
            P("fsdp", None),
            P(),
            P("fsdp", None),
            P(),
            P(),
            P("fsdp", None),
            P(),
            P("fsdp", None),
            P(),
        ),
        out_specs=(
            P("fsdp", "seq", None),
            P("fsdp", "seq", None),
            P(),
            P("fsdp", None),
            P(),
            P("fsdp", None),
            P(),
            P(),
            P("fsdp", None),
            P(),
            P("fsdp", None),
            P(),
        ),
        check_vma=False,
    )
```

profile of v0, /device:TPU:0, one launch (start us, length us, event | category | flops | bytes accessed | tf_op | source)
XLA Modules:
  0.0 1041.5 jit_solution(17890892516380688609)
XLA Ops:
  15.6 63.1 %all-gather.5.cloned.1.call-done = bf16[768,2304]{1,0:T(8,128)(2,1)} async-done(((bf16[96,2304]{1,0:T(8,128)(2,1)}), bf16[768,2304]{1,0:T(8,128)(2,1)}) %all-gather.5.cloned.1.call-update) | async-done | bytes 3538960 | tf_op jit(solution)/shard_map/all_gather | solution.py:64
  85.3 9.1 reshape.215
  94.4 7.9 copy.69
  113.0 34.3 %all-to-all-done = bf16[3,256,4,576]{1,3,0,2:T(8,128)(2,1)S(1)} async-done(((bf16[3,256,4,576]{1,3,0,2:T(8,128)(2,1)}), bf16[3,256,4,576]{1,3,0,2:T(8,128)(2,1)S(1)}, u32[]{:S(2)}, u32[]{:S(2)}) %all-to-all-start) | async-done | bytes 3538976 | tf_op jit(solution)/shard_map/all_to_all | solution.py:79
  159.8 9.2 fusion.57
  169.0 10.1 fusion.1
  179.0 9.0 fusion.28
  190.7 10.6 %fusion.58 = (f32[3,3,512]{2,1,0:T(4,128)}, f32[3,3,512,1024]{3,2,1,0:T(8,128)}) fusion(bf16[3,1024,3,3,64]{1,4,3,2,0:T(8,128)(2,1)S(1)} %reshape.216, bf16[3,1024,3,64]{1,3,2,0:T(8,128)(2,1)} %copy-done.13, pred[3,512,1024]{2,1,0:T(8,128)(4,1)} %get-tuple-element.34), kind=kOutput, calls=%fused_computation.122 | convolution fusion | flops 618130944 | bytes 22235136 | tf_op jit(solution)/shard_map/bqhe,bkhe->bhqk/dot_general | solution.py:25
  201.3 10.0 fusion
  211.3 9.0 fusion.29
  225.7 28.3 %all_to_all.60 = bf16[3,1024,192]{2,0,1:T(4,128)(2,1)S(1)} all-to-all(bf16[3,1024,192]{2,0,1:T(4,128)(2,1)S(1)} %pad_maximum_fusion.3), channel_id=1, replica_groups=mesh['fsdp'=8,'seq'=4] {'seq'}, dimensions={1} | all-to-all | bytes 2359296 | tf_op jit(solution)/shard_map/all_to_all | solution.py:106
  265.6 10.9 %fusion.51 = f32[768,3072]{1,0:T(8,128)} fusion(bf16[768,3072]{1,0:T(8,128)(2,1)} %all-gather.9.cloned.1.call-done, f32[768]{0:T(1024)S(1)} %copy-done.25, f32[768]{0:T(1024)S(1)} %fusion.48, f32[768,1]{1,0:T(8,128)} %copy-done.11, f32[768,767]{1,0:T(8,128)} %copy-done.4), kind=kOutput, calls=%fused_computation.117 | convolution fusion | flops 3626237952 | bytes 16521216 | tf_op jit(solution)/shard_map/dot_general | solution.py:112
  282.0 13.7 %convert_reduce_fusion = (f32[3072]{0:T(1024)}, bf16[768,3072]{1,0:T(8,128)(2,1)S(1)}) fusion(f32[768,3072]{1,0:T(8,128)} %fusion.51, f32[3072]{0:T(1024)} %param.23, bf16[768,767]{1,0:T(8,128)(2,1)} %bitcast.116, bf16[3072,767]{1,0:T(8,128)(2,1)} %all-gather.11.cloned.1.call-done), kind=kOutput, calls=%fused_computation.27 | convolution fusion | flops 3673420800 | bytes 20070912 | tf_op jit(solution)/shard_map/tc,fc->tf/dot_general | solution.py:126
  325.3 8.9 all-to-all-done.2
  341.2 8.6 fusion.11
  349.9 15.6 %multiply_reduce_fusion = (f32[3,3,512]{2,1,0:T(4,128)S(1)}, f32[3,3,512,1024]{3,2,1,0:T(8,128)}) fusion(f32[3,3,512,1024]{3,2,1,0:T(8,128)} %get-tuple-element.41, f32[3,3,512]{2,1,0:T(4,128)S(1)} %copy-done.21, bf16[3,1024,3,3,64]{1,4,3,2,0:T(8,128)(2,1)S(1)} %reshape.216, bf16[3,1024,3,64]{1,3,2,0:T(8,128)(2,1)S(1)} %copy-done.8), kind=kOutput, calls=%fused_computation.1 | convolution fusion | flops 618130944 | bytes 39561216 | tf_op jit(solution)/shard_map/bqhe,bkhe->bhqk/dot_general | solution.py:155
  365.5 15.5 %multiply_reduce_fusion.1 = (f32[3,3,512]{2,1,0:T(4,128)S(1)}, f32[3,3,512,1024]{3,2,1,0:T(8,128)}) fusion(f32[3,3,512,1024]{3,2,1,0:T(8,128)} %get-tuple-element.43, f32[3,3,512]{2,1,0:T(4,128)S(1)} %copy-done.22, bf16[3,1024,3,3,64]{1,4,3,2,0:T(8,128)(2,1)S(1)} %reshape.216, bf16[3,1024,3,64]{1,3,2,0:T(8,128)(2,1)S(1)} %copy-done.8), kind=kOutput, calls=%fused_computation.4 | convolution fusion | flops 618130944 | bytes 39561216 | tf_op jit(solution)/shard_map/bqhe,bkhe->bhqk/dot_general | solution.py:155
  381.0 13.1 %multiply_convert_fusion.1 = bf16[3,3,512,1024]{3,2,1,0:T(8,128)(2,1)S(1)} fusion(f32[3,3,512,1024]{3,2,1,0:T(8,128)} %get-tuple-element.48, f32[3,3,512,1024]{3,2,1,0:T(8,128)} %get-tuple-element.43, f32[3,3,512]{2,1,0:T(4,128)S(1)} %get-tuple-element.47, f32[3,3,512]{2,1,0:T(4,128)S(1)} %copy-done.22), kind=kLoop, calls=%fused_computation.3 | loop fusion | flops 18874368 | bytes 47222784 | tf_op jit(solution)/shard_map/convert_element_type | solution.py:159
  399.0 8.3 fusion.24
  407.2 13.1 %multiply_convert_fusion = bf16[3,3,512,1024]{3,2,1,0:T(8,128)(2,1)S(1)} fusion(f32[3,3,512,1024]{3,2,1,0:T(8,128)} %get-tuple-element.50, f32[3,3,512,1024]{3,2,1,0:T(8,128)} %get-tuple-element.41, f32[3,3,512]{2,1,0:T(4,128)S(1)} %get-tuple-element.49, f32[3,3,512]{2,1,0:T(4,128)S(1)} %copy-done.21), kind=kLoop, calls=%fused_computation | loop fusion | flops 18874368 | bytes 47222784 | tf_op jit(solution)/shard_map/convert_element_type | solution.py:159
  432.4 63.3 %all_to_all.61 = bf16[3,1024,576]{2,0,1:T(4,128)(2,1)S(1)} all-to-all(bf16[3,1024,576]{2,0,1:T(4,128)(2,1)} %copy.82), channel_id=1, replica_groups=mesh['fsdp'=8,'seq'=4] {'seq'}, dimensions={1} | all-to-all | bytes 7077888 | tf_op jit(solution)/shard_map/all_to_all | solution.py:173
  502.3 8.0 reshape.222
  510.3 7.6 fusion.49
  519.2 13.5 %fusion.52 = f32[3072,767]{1,0:T(8,128)} fusion(bf16[768,767]{1,0:T(8,128)(2,1)S(1)} %bitcast.117, f32[768,3072]{1,0:T(8,128)} %fusion.51, f32[3072]{0:T(1024)} %param.23), kind=kOutput, calls=%fused_computation.118 | convolution fusion | flops 3642753024 | bytes 20052480 | tf_op jit(solution)/shard_map/tf,tc->fc/dot_general | solution.py:124
  532.8 10.8 %fusion.50 = f32[768,3072]{1,0:T(8,128)} fusion(bf16[768,3072]{1,0:T(8,128)(2,1)} %copy-done.15, f32[768]{0:T(1024)S(1)} %copy-done.25, f32[768]{0:T(1024)S(1)} %fusion.48, f32[768,1]{1,0:T(8,128)} %copy-done.11, f32[768,767]{1,0:T(8,128)} %copy-done.4), kind=kOutput, calls=%fused_computation.116 | convolution fusion | flops 3626237952 | bytes 16521216 | tf_op jit(solution)/shard_map/td,tf->df/dot_general | solution.py:129
  544.8 12.8 %add_convert_fusion.2 = bf16[768,767]{1,0:T(8,128)(2,1)} fusion(f32[768,767]{1,0:T(8,128)} %copy-done.4, bf16[3072,767]{1,0:T(8,128)(2,1)} %all-gather.11.cloned.1.call-done, f32[767]{0:T(1024)S(1)} %copy-done.38, f32[768,3072]{1,0:T(8,128)} %fusion.51, f32[3072]{0:T(1024)} %param.23), kind=kOutput, calls=%fused_computation.55 | convolution fusion | flops 3644520192 | bytes 17699324 | tf_op jit(solution)/shard_map/dot_general | solution.py:114
  560.5 8.2 multiply_reduce_fusion.3
  568.7 39.5 %all-reduce = (f32[768]{0:T(1024)}, f32[12,128]{1,0:T(8,128)}, f32[767]{0:T(1024)}, f32[768]{0:T(1024)}, f32[3072]{0:T(1024)}, /*index=5*/f32[767]{0:T(1024)}) all-reduce(f32[768]{0:T(1024)} %get-tuple-element.14, f32[12,128]{1,0:T(8,128)} %pad_maximum_fusion.5, ...), channel_id=1, replica_groups=mesh['fsdp'=8,'seq'=4] {'fsdp','seq'}, use_global_device_ids=true, to_apply=%region_15.16 | all-reduce | flops 7678 | bytes 61424 | tf_op jit(solution)/shard_map/psum | solution.py:194
  610.6 34.1 %reduce-scatter.5.cloned.1.call-done = f32[96,2304]{1,0:T(8,128)} async-done(((f32[768,2304]{1,0:T(8,128)}), f32[96,2304]{1,0:T(8,128)}) %reduce-scatter.5.cloned.1.call-update) | async-done | bytes 884752 | tf_op jit(solution)/shard_map/reduce_scatter | solution.py:183
  646.6 164.6 %reduce-scatter.11.cloned.1.call-done = f32[384,767]{1,0:T(8,128)} async-done(((f32[3072,767]{1,0:T(8,128)}), f32[384,767]{1,0:T(8,128)}) %reduce-scatter.11.cloned.1.call-update) | async-done | bytes 1178128 | tf_op jit(solution)/shard_map/reduce_scatter | solution.py:186
  813.4 164.5 %reduce-scatter.9.cloned.1.call-done = f32[96,3072]{1,0:T(8,128)} async-done(((f32[768,3072]{1,0:T(8,128)}), f32[96,3072]{1,0:T(8,128)}) %reduce-scatter.9.cloned.1.call-update) | async-done | bytes 1179664 | tf_op jit(solution)/shard_map/reduce_scatter | solution.py:185
  984.6 42.9 %all-reduce.4.cloned.1.call-done = (bf16[96,2304]{1,0:T(8,128)(2,1)}, bf16[96,767]{1,0:T(8,128)(2,1)}, bf16[96,3072]{1,0:T(8,128)(2,1)}, bf16[384,767]{1,0:T(8,128)(2,1)}) async-done(((bf16[96,2304]{1,0:T(8,128)(2,1)}, bf16[96,767]{1,0:T(8,128)(2,1)}, bf16[96,3072]{1,0:T(8,128)(2,1)}, bf16[384,767]{1,0:T(8,128)(2,1)}), (bf16[96,2304]{1,0:T(8,128)(2,1)}, bf16[96,767]{1,0:T(8,128)(2,1)}, ...) | async-done | bytes 1768528 | tf_op jit(solution)/shard_map/psum | solution.py:189
  (180 shorter events, 148.7 us)
Async XLA Ops:
  7.2 4.9 copy-start.16
  7.2 71.5 %all-gather.5.cloned.1.call-start = ((), (), s32[]{:S(2)}) async-start(), calls=%async_computation.8 | async-start | bytes 3981312 | tf_op jit(solution)/shard_map/all_gather | solution.py:64
  9.4 251.2 %all-gather.7.cloned.1.call-start = ((), (), s32[]{:S(2)}) async-start(), calls=%async_computation.9 | async-start | bytes 1327104 | tf_op jit(solution)/shard_map/all_gather | solution.py:65
  11.1 254.5 %all-gather.9.cloned.1.call-start = ((), (), s32[]{:S(2)}) async-start(), calls=%async_computation.10 | async-start | bytes 5308416 | tf_op jit(solution)/shard_map/all_gather | solution.py:66
  12.9 65.9 %copy-start.9 = (f32[1,768]{0,1:T(8,128)}, f32[1,768]{0,1:T(8,128)S(1)}, u32[]{:S(2)}) copy-start(f32[1,768]{0,1:T(8,128)S(1)} %copy.93) | copy-start | bytes 9220
  12.9 65.8 %copy-start.26 = (f32[768]{0:T(1024)S(1)}, f32[768]{0:T(1024)}, u32[]{:S(2)}) copy-start(f32[768]{0:T(1024)} %param.16) | copy-start | bytes 9220
  14.5 70.8 %copy-start = (f32[768,767]{1,0:T(8,128)}, f32[768,767]{1,0:T(8,128)S(1)}, u32[]{:S(2)}) copy-start(f32[768,767]{1,0:T(8,128)S(1)} %convert.50) | copy-start | bytes 7068676
  15.6 69.7 %copy-start.23 = (f32[768]{0:T(1024)}, f32[768]{0:T(1024)S(1)}, u32[]{:S(2)}) copy-start(f32[768]{0:T(1024)S(1)} %fusion.47) | copy-start | bytes 9220
  102.3 45.0 %all-to-all-start = ((bf16[3,256,4,576]{1,3,0,2:T(8,128)(2,1)}), bf16[3,256,4,576]{1,3,0,2:T(8,128)(2,1)S(1)}, u32[]{:S(2)}, u32[]{:S(2)}) async-start(bf16[3,256,4,576]{1,3,0,2:T(8,128)(2,1)} %copy.69), calls=%async_computation | async-start | bytes 7077888 | tf_op jit(solution)/shard_map/all_to_all | solution.py:79
  106.1 175.9 %all-gather.11.cloned.1.call-start = ((), (), s32[]{:S(2)}) async-start(), calls=%async_computation.11 | async-start | bytes 5308416 | tf_op jit(solution)/shard_map/all_gather | solution.py:67
  158.0 11.0 %copy-start.13 = (bf16[3,1024,3,64]{1,3,2,0:T(8,128)(2,1)}, bf16[3,1024,3,64]{1,3,2,0:T(8,128)(2,1)S(1)}, u32[]{:S(2)}) copy-start(bf16[3,1024,3,64]{1,3,2,0:T(8,128)(2,1)S(1)} %slice_bitcast_fusion.1) | copy-start | bytes 3538948
  254.0 6.6 copy-start.37
  282.0 13.7 %copy-start.5 = (f32[768,767]{1,0:T(8,128)S(1)}, f32[768,767]{1,0:T(8,128)}, u32[]{:S(2)}) copy-start(f32[768,767]{1,0:T(8,128)} %copy-done.4) | copy-start | bytes 7068676
  282.0 13.7 %copy-start.12 = (f32[768,1]{1,0:T(8,128)S(1)}, f32[768,1]{1,0:T(8,128)}, u32[]{:S(2)}) copy-start(f32[768,1]{1,0:T(8,128)} %copy-done.11) | copy-start | bytes 9220
  282.0 13.7 %copy-start.35 = (bf16[768,3072]{1,0:T(8,128)(2,1)S(1)}, bf16[768,3072]{1,0:T(8,128)(2,1)}, u32[]{:S(2)}) copy-start(bf16[768,3072]{1,0:T(8,128)(2,1)} %all-gather.9.cloned.1.call-done) | copy-start | bytes 14155780
  295.7 4.8 copy-start.15
  314.0 20.2 %all-to-all-start.2 = ((bf16[3,256,4,192]{1,3,0,2:T(8,128)(2,1)}), bf16[3,256,4,192]{1,3,0,2:T(8,128)(2,1)}, u32[]{:S(2)}, u32[]{:S(2)}) async-start(bf16[3,256,4,192]{1,3,0,2:T(8,128)(2,1)} %copy.79), calls=%async_computation.2 | async-start | bytes 2359296 | tf_op jit(solution)/shard_map/all_to_all | solution.py:144
  318.3 290.7 %reduce-scatter.7.cloned.1.call-start = ((), (), s32[]{:S(2)}) async-start(), calls=%async_computation.13 | async-start | bytes 2654208 | tf_op jit(solution)/shard_map/reduce_scatter | solution.py:184
  325.2 319.5 %reduce-scatter.5.cloned.1.call-start = ((), (), s32[]{:S(2)}) async-start(), calls=%async_computation.12 | async-start | bytes 7962624 | tf_op jit(solution)/shard_map/reduce_scatter | solution.py:183
  341.2 8.6 copy-start.8
  341.2 8.7 copy-start.21
  349.9 15.7 %copy-start.22 = (f32[3,3,512]{2,1,0:T(4,128)S(1)}, f32[3,3,512]{2,1,0:T(4,128)}, u32[]{:S(2)}) copy-start(f32[3,3,512]{2,1,0:T(4,128)} %log_add_fusion.1) | copy-start | bytes 55300
  502.3 8.0 copy-start.1
  502.3 8.0 copy-start.10
  502.3 8.0 copy-start.24
  502.3 8.0 copy-start.27
  518.0 293.3 %reduce-scatter.11.cloned.1.call-start = ((), (), s32[]{:S(2)}) async-start(), calls=%async_computation.15 | async-start | bytes 10616832 | tf_op jit(solution)/shard_map/reduce_scatter | solution.py:186
  532.7 445.1 %reduce-scatter.9.cloned.1.call-start = ((), (), s32[]{:S(2)}) async-start(), calls=%async_computation.14 | async-start | bytes 10616832 | tf_op jit(solution)/shard_map/reduce_scatter | solution.py:185
  543.6 484.0 %all-reduce.4.cloned.1.call-start = ((), (), s32[]{:S(2)}) async-start(), calls=%async_computation.16 | async-start | bytes 3538944 | tf_op jit(solution)/shard_map/psum | solution.py:189
  560.5 8.2 copy-start.33
  560.5 47.7 %copy-start.31 = (f32[768]{0:T(1024)S(1)}, f32[768]{0:T(1024)}, u32[]{:S(2)}) copy-start(f32[768]{0:T(1024)} %copy-done.30) | copy-start | bytes 9220
  1027.6 5.9 copy-start.20
  (18 other events, 34.9 us)
Sparse Core Ops, SparseCore 0:
  10.8 67.8 all-gather.4
  81.5 39.5 all-gather.6
  123.2 78.6 all-gather.8
  204.0 77.9 all-gather.10
  325.3 67.4 reduce-scatter.6
  518.1 126.5 reduce-scatter.4
  648.7 162.5 reduce-scatter.10
  815.3 162.5 reduce-scatter.8
  981.8 45.7 all-reduce.3
where the time goes:
time: 1050 us; the launch traced here: 1040 us
  waiting for transfers between devices  518 us (49%)
  matrix products  194 us (18%)
  blocking collectives  131 us (12%)
  other arithmetic  96.7 us (9%)
  local copies, waits for them, and re-layouts  78 us (7%)
  between operations  14.8 us (1%)
    reduce_scatter x1, waiting for transfers between devices, local(): lax.psum_scatter(proj_grad, 'fsdp', scatter_dimension=0, tiled=True)  165 us
    reduce_scatter x1, waiting for transfers between devices, local(): lax.psum_scatter(fc_grad, 'fsdp', scatter_dimension=0, tiled=True)  164 us
    all_to_all x1, blocking collectives, local(): lax.all_to_all(d_packed, 'seq', split_axis=1, concat_axis=2, tiled=True)  63.3 us
    all_gather x1, waiting for transfers between devices, local(): lax.all_gather(qkv_weight.astype(jnp.bfloat16), 'fsdp', axis=0, tiled=True)  63.1 us
    psum x1, waiting for transfers between devices, local(): lax.psum(qkv_share.astype(jnp.bfloat16), 'seq').astype(jnp.float32)  42.9 us
    psum x1, blocking collectives, local(): lax.psum((gain_one_grad, qv_bias_grad, out_bias_grad, gain_two_grad, fc_b...  39.5 us
    all_to_all x1, waiting for transfers between devices, local(): lax.all_to_all(packed, 'seq', split_axis=2, concat_axis=1, tiled=True)  34.3 us
    reduce_scatter x1, waiting for transfers between devices, local(): lax.psum_scatter(qkv_grad, 'fsdp', scatter_dimension=0, tiled=True)  34.1 us
  transfers between devices with their start and end apart: 11, of which 8 were waited for; matrix products, arithmetic and copies ran while one was open for 31% of the time, Pallas kernels for 0%

commit v1 on v0

--- a/solution.py
+++ b/solution.py
@@ -5,6 +5,10 @@
 from jax.sharding import PartitionSpec as P
 
 EPS = 1e-06
+
+
+def test_clusters(mine):
+    return jnp.sum(jax.lax.all_gather(mine, "seq"), axis=0)
 
 
 def centred_norm(residual, gain):
@@ -186,7 +190,7 @@
         lax.psum_scatter(proj_grad, "fsdp", scatter_dimension=0, tiled=True),
     )
     qkv_share, out_share, fc_share, proj_share = (
-        lax.psum(qkv_share.astype(jnp.bfloat16), "seq").astype(jnp.float32),
+        test_clusters(qkv_share.astype(jnp.bfloat16)).astype(jnp.float32),
         lax.psum(out_share.astype(jnp.bfloat16), "seq").astype(jnp.float32),
         lax.psum(fc_share.astype(jnp.bfloat16), "seq").astype(jnp.float32),
         lax.psum(proj_share.astype(jnp.bfloat16), "seq").astype(jnp.float32),

time: 1050 us -> 932 us (0.89)
  waiting for transfers between devices: 518 us -> 386 us
    reduce_scatter x1, waiting for transfers between devices: 165 us -> 0.01 us  [local(): lax.psum_scatter(proj_grad, 'fsdp', scatter_dimension=0, tiled=True)]
    reduce_scatter x1, waiting for transfers between devices: 34.1 us -> 129 us  [local(): lax.psum_scatter(qkv_grad, 'fsdp', scatter_dimension=0, tiled=True)]
    psum x1, waiting for transfers between devices: 42.9 us -> 0.01 us  [local(): lax.psum(out_share.astype(jnp.bfloat16), 'seq').astype(jnp.float32)]
    reduce_scatter x1, waiting for transfers between devices: 164 us -> 142 us  [local(): lax.psum_scatter(fc_grad, 'fsdp', scatter_dimension=0, tiled=True)]
  transfers between devices with their start and end apart: 11 -> 12, of which waited for: 8 -> 6; matrix products, arithmetic and copies ran while one was open for 31% -> 37% of each run, Pallas kernels for 0% -> 0%
where the time goes in v1:
time: 932 us; the launch traced here: 925 us
  waiting for transfers between devices  386 us (41%)
  matrix products  198 us (21%)
  blocking collectives  133 us (14%)
  other arithmetic  99.6 us (11%)
  local copies, waits for them, and re-layouts  83.2 us (9%)
  between operations  15 us (2%)
    reduce_scatter x1, waiting for transfers between devices, local(): lax.psum_scatter(fc_grad, 'fsdp', scatter_dimension=0, tiled=True)  142 us
    reduce_scatter x1, waiting for transfers between devices, local(): lax.psum_scatter(qkv_grad, 'fsdp', scatter_dimension=0, tiled=True)  129 us
    all_to_all x1, blocking collectives, local(): lax.all_to_all(d_packed, 'seq', split_axis=1, concat_axis=2, tiled=True)  63.7 us
    all_gather x1, waiting for transfers between devices, local(): lax.all_gather(qkv_weight.astype(jnp.bfloat16), 'fsdp', axis=0, tiled=True)  63 us
    psum x1, blocking collectives, local(): lax.psum((gain_one_grad, qv_bias_grad, out_bias_grad, gain_two_grad, fc_b...  41.2 us
    all_to_all x1, waiting for transfers between devices, local(): lax.all_to_all(packed, 'seq', split_axis=2, concat_axis=1, tiled=True)  33.9 us
    dot_general x2, matrix products, local(): jnp.einsum('bqhe,bkhe->bhqk', grad_block, value_rows, preferred_element_t...  31.6 us
    all_to_all x1, blocking collectives, local(): lax.all_to_all(attended, 'seq', split_axis=1, concat_axis=2, tiled=True)  28.4 us
  transfers between devices with their start and end apart: 12, of which 6 were waited for; matrix products, arithmetic and copies ran while one was open for 37% of the time, Pallas kernels for 0%

profile of v1, /device:TPU:0, one launch (start us, length us, event | category | flops | bytes accessed | tf_op | source)
XLA Modules:
  0.0 925.0 jit_solution(14397701955618658779)
XLA Ops:
  15.7 63.0 %all-gather.7.cloned.1.call-done = bf16[768,2304]{1,0:T(8,128)(2,1)} async-done(((bf16[96,2304]{1,0:T(8,128)(2,1)}), bf16[768,2304]{1,0:T(8,128)(2,1)}) %all-gather.7.cloned.1.call-update) | async-done | bytes 3538960 | tf_op jit(solution)/shard_map/all_gather | solution.py:68
  78.7 6.6 add_convert_fusion
  85.3 9.1 reshape.215
  94.4 7.9 copy.69
  113.4 33.9 %all-to-all-done = bf16[3,256,4,576]{1,3,0,2:T(8,128)(2,1)S(1)} async-done(((bf16[3,256,4,576]{1,3,0,2:T(8,128)(2,1)}), bf16[3,256,4,576]{1,3,0,2:T(8,128)(2,1)S(1)}, u32[]{:S(2)}, u32[]{:S(2)}) %all-to-all-start) | async-done | bytes 3538976 | tf_op jit(solution)/shard_map/all_to_all | solution.py:83
  159.8 9.2 fusion.57
  169.0 10.1 %fusion.1 = f32[3,3,512]{2,1,0:T(4,128)} fusion(f32[3,3,512,1024]{3,2,1,0:T(8,128)} %get-tuple-element.40, f32[3,3,512]{2,1,0:T(4,128)} %get-tuple-element.39), kind=kLoop, calls=%fused_computation.13 | loop fusion | flops 9432576 | bytes 18911232 | tf_op jit(solution)/shard_map/reduce_sum | solution.py:102
  179.0 9.0 fusion.28
  190.5 10.6 %fusion.58 = (f32[3,3,512]{2,1,0:T(4,128)}, f32[3,3,512,1024]{3,2,1,0:T(8,128)}) fusion(bf16[3,1024,3,3,64]{1,4,3,2,0:T(8,128)(2,1)S(1)} %reshape.216, bf16[3,1024,3,64]{1,3,2,0:T(8,128)(2,1)} %copy-done.17, pred[3,512,1024]{2,1,0:T(8,128)(4,1)} %get-tuple-element.33), kind=kOutput, calls=%fused_computation.122 | convolution fusion | flops 618130944 | bytes 22235136 | tf_op jit(solution)/shard_map/bqhe,bkhe->bhqk/dot_general | solution.py:29
  201.1 10.0 %fusion = f32[3,3,512]{2,1,0:T(4,128)} fusion(f32[3,3,512,1024]{3,2,1,0:T(8,128)} %get-tuple-element.42, f32[3,3,512]{2,1,0:T(4,128)} %get-tuple-element.41), kind=kLoop, calls=%fused_computation.12 | loop fusion | flops 9432576 | bytes 18911232 | tf_op jit(solution)/shard_map/reduce_sum | solution.py:102
  211.1 9.0 fusion.29
  225.5 28.4 %all_to_all.60 = bf16[3,1024,192]{2,0,1:T(4,128)(2,1)S(1)} all-to-all(bf16[3,1024,192]{2,0,1:T(4,128)(2,1)S(1)} %pad_maximum_fusion.3), channel_id=1, replica_groups=mesh['fsdp'=8,'seq'=4] {'seq'}, dimensions={1} | all-to-all | bytes 2359296 | tf_op jit(solution)/shard_map/all_to_all | solution.py:110
  265.4 10.8 %fusion.51 = f32[768,3072]{1,0:T(8,128)} fusion(bf16[768,3072]{1,0:T(8,128)(2,1)} %all-gather.11.cloned.1.call-done, f32[768]{0:T(1024)S(1)} %copy-done.33, f32[768]{0:T(1024)S(1)} %fusion.48, f32[768,1]{1,0:T(8,128)} %copy-done.14, f32[768,767]{1,0:T(8,128)} %copy-done.6), kind=kOutput, calls=%fused_computation.117 | convolution fusion | flops 3626237952 | bytes 16521216 | tf_op jit(solution)/shard_map/dot_general | solution.py:116
  282.0 13.9 %convert_reduce_fusion = (f32[3072]{0:T(1024)}, bf16[768,3072]{1,0:T(8,128)(2,1)S(1)}) fusion(f32[768,3072]{1,0:T(8,128)} %fusion.51, f32[3072]{0:T(1024)} %param.23, bf16[768,767]{1,0:T(8,128)(2,1)} %bitcast.119, bf16[3072,767]{1,0:T(8,128)(2,1)} %all-gather.13.cloned.1.call-done), kind=kOutput, calls=%fused_computation.27 | convolution fusion | flops 3673420800 | bytes 20070912 | tf_op jit(solution)/shard_map/tc,fc->tf/dot_general | solution.py:130
  306.7 13.4 %fusion.52 = f32[3072,767]{1,0:T(8,128)} fusion(bf16[768,767]{1,0:T(8,128)(2,1)} %bitcast.120, f32[768,3072]{1,0:T(8,128)} %fusion.51, f32[3072]{0:T(1024)} %param.23), kind=kOutput, calls=%fused_computation.118 | convolution fusion | flops 3642753024 | bytes 20052480 | tf_op jit(solution)/shard_map/tf,tc->fc/dot_general | solution.py:128
  320.3 10.8 %fusion.50 = f32[768,3072]{1,0:T(8,128)} fusion(bf16[768,3072]{1,0:T(8,128)(2,1)} %copy-done.19, f32[768]{0:T(1024)S(1)} %copy-done.33, f32[768]{0:T(1024)S(1)} %fusion.48, f32[768,1]{1,0:T(8,128)} %copy-done.14, f32[768,767]{1,0:T(8,128)} %copy-done.6), kind=kOutput, calls=%fused_computation.116 | convolution fusion | flops 3626237952 | bytes 16521216 | tf_op jit(solution)/shard_map/td,tf->df/dot_general | solution.py:133
  350.2 12.9 %all-to-all-done.2 = bf16[3,256,4,192]{1,3,0,2:T(8,128)(2,1)} async-done(((bf16[3,256,4,192]{1,3,0,2:T(8,128)(2,1)}), bf16[3,256,4,192]{1,3,0,2:T(8,128)(2,1)}, u32[]{:S(2)}, u32[]{:S(2)}) %all-to-all-start.2) | async-done | bytes 1179680 | tf_op jit(solution)/shard_map/all_to_all | solution.py:148
  369.7 16.0 %multiply_reduce_fusion = (f32[3,3,512]{2,1,0:T(4,128)S(1)}, f32[3,3,512,1024]{3,2,1,0:T(8,128)}) fusion(f32[3,3,512,1024]{3,2,1,0:T(8,128)} %get-tuple-element.40, f32[3,3,512]{2,1,0:T(4,128)} %log_add_fusion, bf16[3,1024,3,3,64]{1,4,3,2,0:T(8,128)(2,1)S(1)} %reshape.216, bf16[3,1024,3,64]{1,3,2,0:T(8,128)(2,1)} %reshape.221), kind=kOutput, calls=%fused_computation.1 | convolution fusion | flops 618130944 | bytes 39561216 | tf_op jit(solution)/shard_map/bqhe,bkhe->bhqk/dot_general | solution.py:159
  385.7 13.0 %multiply_convert_fusion = bf16[3,3,512,1024]{3,2,1,0:T(8,128)(2,1)S(1)} fusion(f32[3,3,512,1024]{3,2,1,0:T(8,128)} %get-tuple-element.49, f32[3,3,512,1024]{3,2,1,0:T(8,128)} %get-tuple-element.40, f32[3,3,512]{2,1,0:T(4,128)S(1)} %get-tuple-element.48, f32[3,3,512]{2,1,0:T(4,128)S(1)} %copy-done.27), kind=kLoop, calls=%fused_computation | loop fusion | flops 18874368 | bytes 47222784 | tf_op jit(solution)/shard_map/convert_element_type | solution.py:163
  405.4 15.6 %multiply_reduce_fusion.1 = (f32[3,3,512]{2,1,0:T(4,128)S(1)}, f32[3,3,512,1024]{3,2,1,0:T(8,128)}) fusion(f32[3,3,512,1024]{3,2,1,0:T(8,128)} %get-tuple-element.42, f32[3,3,512]{2,1,0:T(4,128)S(1)} %copy-done.29, bf16[3,1024,3,3,64]{1,4,3,2,0:T(8,128)(2,1)S(1)} %reshape.216, bf16[3,1024,3,64]{1,3,2,0:T(8,128)(2,1)S(1)} %copy-done.10), kind=kOutput, calls=%fused_computation.4 | convolution fusion | flops 618130944 | bytes 39561216 | tf_op jit(solution)/shard_map/bqhe,bkhe->bhqk/dot_general | solution.py:159
  421.0 13.7 %multiply_convert_fusion.1 = bf16[3,3,512,1024]{3,2,1,0:T(8,128)(2,1)S(1)} fusion(f32[3,3,512,1024]{3,2,1,0:T(8,128)} %get-tuple-element.47, f32[3,3,512,1024]{3,2,1,0:T(8,128)} %get-tuple-element.42, f32[3,3,512]{2,1,0:T(4,128)S(1)} %get-tuple-element.46, f32[3,3,512]{2,1,0:T(4,128)S(1)} %copy-done.29), kind=kLoop, calls=%fused_computation.3 | loop fusion | flops 18874368 | bytes 47222784 | tf_op jit(solution)/shard_map/convert_element_type | solution.py:163
  447.7 6.8 fusion.23
  458.2 8.8 fusion.24
  474.1 63.7 %all_to_all.61 = bf16[3,1024,576]{2,0,1:T(4,128)(2,1)S(1)} all-to-all(bf16[3,1024,576]{2,0,1:T(4,128)(2,1)} %copy.82), channel_id=1, replica_groups=mesh['fsdp'=8,'seq'=4] {'seq'}, dimensions={1} | all-to-all | bytes 7077888 | tf_op jit(solution)/shard_map/all_to_all | solution.py:177
  537.8 6.7 convert_reduce_fusion.1
  544.6 8.0 reshape.222
  552.6 7.6 fusion.49
  564.2 142.0 %reduce-scatter.9.cloned.1.call-done = f32[96,3072]{1,0:T(8,128)} async-done(((f32[768,3072]{1,0:T(8,128)}), f32[96,3072]{1,0:T(8,128)}) %reduce-scatter.9.cloned.1.call-update) | async-done | bytes 1179664 | tf_op jit(solution)/shard_map/reduce_scatter | solution.py:189
  709.5 128.6 %reduce-scatter.5.cloned.1.call-done = f32[96,2304]{1,0:T(8,128)} async-done(((f32[768,2304]{1,0:T(8,128)}), f32[96,2304]{1,0:T(8,128)}) %reduce-scatter.5.cloned.1.call-update) | async-done | bytes 884752 | tf_op jit(solution)/shard_map/reduce_scatter | solution.py:187
  840.1 12.6 %add_convert_fusion.2 = bf16[768,767]{1,0:T(8,128)(2,1)} fusion(f32[768,767]{1,0:T(8,128)} %copy-done.6, bf16[3072,767]{1,0:T(8,128)(2,1)} %all-gather.13.cloned.1.call-done, f32[767]{0:T(1024)S(1)} %copy-done.42, f32[768,3072]{1,0:T(8,128)} %fusion.51, f32[3072]{0:T(1024)} %param.23), kind=kOutput, calls=%fused_computation.55 | convolution fusion | flops 3644520192 | bytes 17699324 | tf_op jit(solution)/shard_map/dot_general | solution.py:118
  855.6 8.2 multiply_reduce_fusion.3
  863.8 41.2 %all-reduce = (f32[768]{0:T(1024)}, f32[12,128]{1,0:T(8,128)}, f32[767]{0:T(1024)}, f32[768]{0:T(1024)}, f32[3072]{0:T(1024)}, /*index=5*/f32[767]{0:T(1024)}) all-reduce(f32[768]{0:T(1024)} %get-tuple-element.14, f32[12,128]{1,0:T(8,128)} %pad_maximum_fusion.5, ...), channel_id=1, replica_groups=mesh['fsdp'=8,'seq'=4] {'fsdp','seq'}, use_global_device_ids=true, to_apply=%region_15.16 | all-reduce | flops 7678 | bytes 61424 | tf_op jit(solution)/shard_map/psum | solution.py:198
  (203 shorter events, 148.9 us)
Async XLA Ops:
  7.2 71.5 %all-gather.7.cloned.1.call-start = ((), (), s32[]{:S(2)}) async-start(), calls=%async_computation.8 | async-start | bytes 3981312 | tf_op jit(solution)/shard_map/all_gather | solution.py:68
  9.4 251.1 %all-gather.9.cloned.1.call-start = ((), (), s32[]{:S(2)}) async-start(), calls=%async_computation.9 | async-start | bytes 1327104 | tf_op jit(solution)/shard_map/all_gather | solution.py:69
  11.1 254.3 %all-gather.11.cloned.1.call-start = ((), (), s32[]{:S(2)}) async-start(), calls=%async_computation.10 | async-start | bytes 5308416 | tf_op jit(solution)/shard_map/all_gather | solution.py:70
  12.9 65.9 %copy-start.12 = (f32[1,768]{0,1:T(8,128)}, f32[1,768]{0,1:T(8,128)S(1)}, u32[]{:S(2)}) copy-start(f32[1,768]{0,1:T(8,128)S(1)} %copy.93) | copy-start | bytes 9220
  12.9 65.8 %copy-start.34 = (f32[768]{0:T(1024)S(1)}, f32[768]{0:T(1024)}, u32[]{:S(2)}) copy-start(f32[768]{0:T(1024)} %param.16) | copy-start | bytes 9220
  14.5 70.8 %copy-start.2 = (f32[768,767]{1,0:T(8,128)}, f32[768,767]{1,0:T(8,128)S(1)}, u32[]{:S(2)}) copy-start(f32[768,767]{1,0:T(8,128)S(1)} %convert.51) | copy-start | bytes 7068676
  15.7 69.6 %copy-start.31 = (f32[768]{0:T(1024)}, f32[768]{0:T(1024)S(1)}, u32[]{:S(2)}) copy-start(f32[768]{0:T(1024)S(1)} %fusion.47) | copy-start | bytes 9220
  102.3 45.0 %all-to-all-start = ((bf16[3,256,4,576]{1,3,0,2:T(8,128)(2,1)}), bf16[3,256,4,576]{1,3,0,2:T(8,128)(2,1)S(1)}, u32[]{:S(2)}, u32[]{:S(2)}) async-start(bf16[3,256,4,576]{1,3,0,2:T(8,128)(2,1)} %copy.69), calls=%async_computation | async-start | bytes 7077888 | tf_op jit(solution)/shard_map/all_to_all | solution.py:83
  106.1 175.9 %all-gather.13.cloned.1.call-start = ((), (), s32[]{:S(2)}) async-start(), calls=%async_computation.11 | async-start | bytes 5308416 | tf_op jit(solution)/shard_map/all_gather | solution.py:71
  108.4 451.9 %reduce-scatter.7.cloned.1.call-start = ((), (), s32[]{:S(2)}) async-start(), calls=%async_computation.13 | async-start | bytes 2654208 | tf_op jit(solution)/shard_map/reduce_scatter | solution.py:188
  157.9 11.0 %copy-start.17 = (bf16[3,1024,3,64]{1,3,2,0:T(8,128)(2,1)}, bf16[3,1024,3,64]{1,3,2,0:T(8,128)(2,1)S(1)}, u32[]{:S(2)}) copy-start(bf16[3,1024,3,64]{1,3,2,0:T(8,128)(2,1)S(1)} %slice_bitcast_fusion.1) | copy-start | bytes 3538948
  282.0 13.9 %copy-start.7 = (f32[768,767]{1,0:T(8,128)S(1)}, f32[768,767]{1,0:T(8,128)}, u32[]{:S(2)}) copy-start(f32[768,767]{1,0:T(8,128)} %copy-done.6) | copy-start | bytes 7068676
  282.0 13.9 %copy-start.15 = (f32[768,1]{1,0:T(8,128)S(1)}, f32[768,1]{1,0:T(8,128)}, u32[]{:S(2)}) copy-start(f32[768,1]{1,0:T(8,128)} %copy-done.14) | copy-start | bytes 9220
  282.0 13.9 %copy-start.40 = (bf16[768,3072]{1,0:T(8,128)(2,1)S(1)}, bf16[768,3072]{1,0:T(8,128)(2,1)}, u32[]{:S(2)}) copy-start(bf16[768,3072]{1,0:T(8,128)(2,1)} %all-gather.11.cloned.1.call-done) | copy-start | bytes 14155780
  306.6 255.3 %reduce-scatter.11.cloned.1.call-start = ((), (), s32[]{:S(2)}) async-start(), calls=%async_computation.15 | async-start | bytes 10616832 | tf_op jit(solution)/shard_map/reduce_scatter | solution.py:190
  320.1 386.1 %reduce-scatter.9.cloned.1.call-start = ((), (), s32[]{:S(2)}) async-start(), calls=%async_computation.14 | async-start | bytes 10616832 | tf_op jit(solution)/shard_map/reduce_scatter | solution.py:189
  342.9 20.2 %all-to-all-start.2 = ((bf16[3,256,4,192]{1,3,0,2:T(8,128)(2,1)}), bf16[3,256,4,192]{1,3,0,2:T(8,128)(2,1)}, u32[]{:S(2)}, u32[]{:S(2)}) async-start(bf16[3,256,4,192]{1,3,0,2:T(8,128)(2,1)} %copy.79), calls=%async_computation.2 | async-start | bytes 2359296 | tf_op jit(solution)/shard_map/all_to_all | solution.py:148
  347.2 490.8 %reduce-scatter.5.cloned.1.call-start = ((), (), s32[]{:S(2)}) async-start(), calls=%async_computation.12 | async-start | bytes 7962624 | tf_op jit(solution)/shard_map/reduce_scatter | solution.py:187
  369.7 16.0 %copy-start.27 = (f32[3,3,512]{2,1,0:T(4,128)S(1)}, f32[3,3,512]{2,1,0:T(4,128)}, u32[]{:S(2)}) copy-start(f32[3,3,512]{2,1,0:T(4,128)} %log_add_fusion) | copy-start | bytes 55300
  434.7 19.8 %slice-start = ((s8[18874368]{0:T(1024)(128)(4,1)}), s8[4194304]{0:T(1024)(128)(4,1)S(1)}, s32[]{:S(2)}) async-start(s8[18874368]{0:T(1024)(128)(4,1)} %bitcast.114), calls=%async_computation.18 | async-start | bytes 8388608
  434.7 19.8 %slice-start.1 = ((s8[18874368]{0:T(1024)(128)(4,1)}), s8[4194304]{0:T(1024)(128)(4,1)S(1)}, s32[]{:S(2)}) async-start(s8[18874368]{0:T(1024)(128)(4,1)} %bitcast.114), calls=%async_computation.19 | async-start | bytes 8388608
  442.0 12.6 %slice-start.2 = ((s8[18874368]{0:T(1024)(128)(4,1)}), s8[4194304]{0:T(1024)(128)(4,1)S(1)}, s32[]{:S(2)}) async-start(s8[18874368]{0:T(1024)(128)(4,1)} %bitcast.114), calls=%async_computation.20 | async-start | bytes 8388608
  442.0 12.6 %slice-start.3 = ((s8[18874368]{0:T(1024)(128)(4,1)}), s8[4194304]{0:T(1024)(128)(4,1)S(1)}, s32[]{:S(2)}) async-start(s8[18874368]{0:T(1024)(128)(4,1)} %bitcast.114), calls=%async_computation.21 | async-start | bytes 8388608
  458.1 8.8 copy-start.16
  458.1 8.8 copy-start.21
  544.6 8.0 copy-start.32
  544.6 8.0 copy-start.35
  560.3 350.0 %all-reduce.4.cloned.1.call-start = ((), (), s32[]{:S(2)}) async-start(), calls=%async_computation.17 | async-start | bytes 2654208 | tf_op jit(solution)/shard_map/psum | solution.py:194
  562.0 146.7 %copy-start.9 = (bf16[3,256,767]{2,1,0:T(8,128)(2,1)S(1)}, bf16[3,256,767]{2,1,0:T(8,128)(2,1)}, u32[]{:S(2)}) copy-start(bf16[3,256,767]{2,1,0:T(8,128)(2,1)} %param.14) | copy-start | bytes 3534340
  708.4 131.7 %copy-start.42 = (f32[767]{0:T(1024)S(1)}, f32[767]{0:T(1024)}, u32[]{:S(2)}) copy-start(f32[767]{0:T(1024)} %param.25) | copy-start | bytes 9208
  708.4 206.8 %all-gather.15.cloned.1.call-start = ((), (), s32[]{:S(2)}) async-start(), calls=%async_computation.16 | async-start | bytes 2211840 | tf_op jit(solution)/shard_map/all_gather | solution.py:11
  855.6 49.4 %copy-start.37 = (f32[768]{0:T(1024)S(1)}, f32[768]{0:T(1024)}, u32[]{:S(2)}) copy-start(f32[768]{0:T(1024)} %copy-done.36) | copy-start | bytes 9220
  (28 other events, 103.2 us)
Sparse Core Ops, SparseCore 0:
  10.8 67.8 all-gather.6
  81.5 39.5 all-gather.8
  123.2 78.6 all-gather.10
  204.0 78.0 all-gather.12
  306.7 67.2 reduce-scatter.6
  377.5 162.4 reduce-scatter.10
  543.6 162.5 reduce-scatter.8
  709.9 128.0 reduce-scatter.4
  841.9 39.4 all-reduce.3
  882.9 20.8 all-gather.14
